TPU v7x, 32 devices: a whole 2x2x4 slice. The times are simulated.
32 devices in a mesh: prec: 16 (over z, x, core), run: 2 (over y).
Axes of the slice: x: 2, y: 2, z: 4, core: 2. Of those that a mesh axis runs over, the one named last changes fastest.
Arguments:
- intensity: bfloat16 [1024, 32768], P('run', 'prec'), may hold values from -6 to 6
- observed: int32 [1024, 4096], P('run', 'prec'), may hold values from 0 to 255, as said below
- run_factors: bfloat16 [1024, 64], P('run'), as said below
- prec_factors: bfloat16 [32768, 64], P('prec'), as said below
Outputs:
- completed: bfloat16 [1024, 32768], P('run', 'prec')
Inputs may be any that keep to these rules, and one draw needn't show every extreme that they name: `observed`: each word packs eight observation flags in its low 8 bits: bit b of word j is the flag of precursor 8 j + b. `run_factors`: rows of the starting factors have scales that vary along the rows. `prec_factors`: rows of the starting factors have scales that vary along the rows.
All inputs are finite; a program needn't handle non-finite values.
Results may differ from a plain program's by a relative error of at most 0.005.
Values may be sent and summed in bfloat16 or wider, within the bound.
A program may use at most 64 MiB of HBM per device.

v0:
```python
import jax
import jax.numpy as jnp
from jax import lax
from jax.sharding import PartitionSpec as P

ITERS = 4


ridge_value = 16.0


def unpack_mask(words):
    shifts = jnp.arange(8, dtype=jnp.int32)
    bits = jnp.right_shift(words[:, :, None], shifts) & 1
    return bits.reshape(words.shape[0], -1).astype(jnp.float32)


def ridge_solve(matrix, gram):
    size = gram.shape[0]
    factor = jnp.linalg.cholesky(gram + ridge_value * jnp.eye(size, dtype=jnp.float32))
    return jax.scipy.linalg.cho_solve((factor, True), matrix.T).T


def inner_gram(factors):
    return lax.dot_general(
        factors, factors, (((0,), (0,)), ((), ())), preferred_element_type=jnp.float32
    )


def masked_resid(intensity, maskf, u_now, v_now):
    fit = jnp.dot(u_now, v_now.T, preferred_element_type=jnp.float32)
    return (maskf * (intensity.astype(jnp.float32) - fit)).astype(jnp.bfloat16)


def local(intensity, observed, run_factors, prec_factors):
    maskf = unpack_mask(observed)
    u_now = run_factors
    v_now = prec_factors
    for step in range(ITERS):
        resid = masked_resid(intensity, maskf, u_now, v_now)
        proj_part = jnp.dot(resid, v_now, preferred_element_type=jnp.float32)
        gram_part = inner_gram(v_now)
        gram_v = lax.psum(gram_part, "prec")
        share = lax.psum_scatter(proj_part, "prec", scatter_dimension=0, tiled=True)
        count = share.shape[0]
        first = lax.axis_index("prec") * count
        mine = lax.dynamic_slice_in_dim(u_now, first, count, 0)
        total = jnp.dot(mine.astype(jnp.float32), gram_v, precision=lax.Precision.HIGHEST) + share
        fresh = ridge_solve(total, gram_v).astype(jnp.bfloat16)
        u_now = lax.all_gather(fresh, "prec", axis=0, tiled=True)
        resid = masked_resid(intensity, maskf, u_now, v_now)
        proj_part = lax.dot_general(
            resid, u_now, (((0,), (0,)), ((), ())), preferred_element_type=jnp.float32
        )
        gram_part = inner_gram(u_now)
        proj_v, gram_u = (
            lax.psum(proj_part.astype(jnp.bfloat16), "run").astype(jnp.float32),
            lax.psum(gram_part.astype(jnp.bfloat16), "run").astype(jnp.float32),
        )
        total = jnp.dot(v_now.astype(jnp.float32), gram_u, precision=lax.Precision.HIGHEST) + proj_v
        v_now = ridge_solve(total, gram_u).astype(jnp.bfloat16)
    fit = jnp.dot(u_now, v_now.T, preferred_element_type=jnp.float32)
    return (maskf * intensity.astype(jnp.float32) + (1.0 - maskf) * fit).astype(jnp.bfloat16)


def solution(mesh):
    return jax.shard_map(
        local,
        mesh=mesh,
        in_specs=(P("run", "prec"), P("run", "prec"), P("run", None), P("prec", None)),
        out_specs=P("run", "prec"),
        check_vma=False,
    )
```

profile of v0, /device:TPU:0, one launch (start us, length us, event | category | flops | bytes accessed | tf_op | source)
XLA Modules:
  0.0 746.3 jit_solution(6776300041927255322)
XLA Ops:
  10.3 5.5 copy.22
  20.7 63.0 %psum.84 = f32[64,64]{0,1:T(8,128)S(1)} all-reduce(f32[64,64]{0,1:T(8,128)S(1)} %fusion.103), channel_id=1, replica_groups=mesh['prec'=16,'run'=2] {'prec'}, use_global_device_ids=true, to_apply=%region_0.0 | all-reduce | flops 4096 | bytes 32768 | tf_op jit(solution)/shard_map/psum | solution.py:43
  83.7 5.8 cholesky.134
  90.9 4.9 custom-call.18
  97.3 17.5 %all_gather.12 = bf16[512,64]{1,0:T(8,128)(2,1)S(1)} all-gather(bf16[32,64]{1,0:T(8,128)(2,1)S(1)} %fusion.31), channel_id=1, replica_groups=mesh['prec'=16,'run'=2] {'prec'}, dimensions={0}, use_global_device_ids=true | all-gather | bytes 69632 | tf_op jit(solution)/shard_map/all_gather | solution.py:50
  119.3 8.2 %psum.85 = bf16[64,64]{0,1:T(8,128)(2,1)S(1)} all-reduce(bf16[64,64]{0,1:T(8,128)(2,1)S(1)} %convolution_convert_fusion.11), channel_id=1, replica_groups=mesh['prec'=16,'run'=2] {'run'}, use_global_device_ids=true, to_apply=%region_4.7 | all-reduce | flops 4096 | bytes 16384 | tf_op jit(solution)/shard_map/psum | solution.py:58
  127.6 5.9 cholesky.145
  134.8 4.9 custom-call.19
  139.7 15.1 %all-reduce.5.cloned.1.call-done = bf16[2048,64]{0,1:T(8,128)(2,1)} async-done(((bf16[2048,64]{0,1:T(8,128)(2,1)}), bf16[2048,64]{0,1:T(8,128)(2,1)}) %all-reduce.5.cloned.1.call-update) | async-done | bytes 262160 | tf_op jit(solution)/shard_map/psum | solution.py:57
  161.7 60.9 %psum.87 = f32[64,64]{0,1:T(8,128)S(1)} all-reduce(f32[64,64]{0,1:T(8,128)S(1)} %fusion.104), channel_id=1, replica_groups=mesh['prec'=16,'run'=2] {'prec'}, use_global_device_ids=true, to_apply=%region_6.0 | all-reduce | flops 4096 | bytes 32768 | tf_op jit(solution)/shard_map/psum | solution.py:43
  222.7 5.8 cholesky.156
  230.0 4.9 custom-call.20
  234.9 46.6 %reduce-scatter.7.cloned.1.call-done = f32[32,64]{1,0:T(8,128)} async-done(((f32[512,64]{1,0:T(8,128)}), f32[32,64]{1,0:T(8,128)}) %reduce-scatter.7.cloned.1.call-update) | async-done | bytes 8208 | tf_op jit(solution)/shard_map/reduce_scatter | solution.py:44
  282.9 19.8 %all_gather.13 = bf16[512,64]{1,0:T(8,128)(2,1)S(1)} all-gather(bf16[32,64]{1,0:T(8,128)(2,1)S(1)} %fusion.32), channel_id=1, replica_groups=mesh['prec'=16,'run'=2] {'prec'}, dimensions={0}, use_global_device_ids=true | all-gather | bytes 69632 | tf_op jit(solution)/shard_map/all_gather | solution.py:50
  307.4 8.1 %psum.88 = bf16[64,64]{0,1:T(8,128)(2,1)S(1)} all-reduce(bf16[64,64]{0,1:T(8,128)(2,1)S(1)} %convolution_convert_fusion.10), channel_id=1, replica_groups=mesh['prec'=16,'run'=2] {'run'}, use_global_device_ids=true, to_apply=%region_8.0 | all-reduce | flops 4096 | bytes 16384 | tf_op jit(solution)/shard_map/psum | solution.py:58
  315.7 5.8 cholesky.167
  322.8 4.9 custom-call.21
  327.7 19.0 %all-reduce.7.cloned.1.call-done = bf16[2048,64]{1,0:T(8,128)(2,1)} async-done(((bf16[2048,64]{1,0:T(8,128)(2,1)}), bf16[2048,64]{1,0:T(8,128)(2,1)}) %all-reduce.7.cloned.1.call-update) | async-done | bytes 262160 | tf_op jit(solution)/shard_map/psum | solution.py:57
  354.5 61.0 %psum.90 = f32[64,64]{0,1:T(8,128)S(1)} all-reduce(f32[64,64]{0,1:T(8,128)S(1)} %fusion.105), channel_id=1, replica_groups=mesh['prec'=16,'run'=2] {'prec'}, use_global_device_ids=true, to_apply=%region_10.0 | all-reduce | flops 4096 | bytes 32768 | tf_op jit(solution)/shard_map/psum | solution.py:43
  415.6 5.8 cholesky.178
  427.8 46.6 %reduce-scatter.9.cloned.1.call-done = f32[32,64]{1,0:T(8,128)} async-done(((f32[512,64]{1,0:T(8,128)}), f32[32,64]{1,0:T(8,128)}) %reduce-scatter.9.cloned.1.call-update) | async-done | bytes 8208 | tf_op jit(solution)/shard_map/reduce_scatter | solution.py:44
  475.7 20.0 %all_gather.14 = bf16[512,64]{1,0:T(8,128)(2,1)S(1)} all-gather(bf16[32,64]{1,0:T(8,128)(2,1)S(1)} %fusion.33), channel_id=1, replica_groups=mesh['prec'=16,'run'=2] {'prec'}, dimensions={0}, use_global_device_ids=true | all-gather | bytes 69632 | tf_op jit(solution)/shard_map/all_gather | solution.py:50
  500.5 8.1 %psum.91 = bf16[64,64]{0,1:T(8,128)(2,1)S(1)} all-reduce(bf16[64,64]{0,1:T(8,128)(2,1)S(1)} %convolution_convert_fusion.9), channel_id=1, replica_groups=mesh['prec'=16,'run'=2] {'run'}, use_global_device_ids=true, to_apply=%region_12.0 | all-reduce | flops 4096 | bytes 16384 | tf_op jit(solution)/shard_map/psum | solution.py:58
  508.7 5.8 cholesky.189
  520.8 19.0 %all-reduce.9.cloned.1.call-done = bf16[2048,64]{1,0:T(8,128)(2,1)} async-done(((bf16[2048,64]{1,0:T(8,128)(2,1)}), bf16[2048,64]{1,0:T(8,128)(2,1)}) %all-reduce.9.cloned.1.call-update) | async-done | bytes 262160 | tf_op jit(solution)/shard_map/psum | solution.py:57
  547.6 61.0 %psum.93 = f32[64,64]{0,1:T(8,128)S(1)} all-reduce(f32[64,64]{0,1:T(8,128)S(1)} %fusion.106), channel_id=1, replica_groups=mesh['prec'=16,'run'=2] {'prec'}, use_global_device_ids=true, to_apply=%region_14.0 | all-reduce | flops 4096 | bytes 32768 | tf_op jit(solution)/shard_map/psum | solution.py:43
  608.7 5.8 cholesky.200
  620.9 46.6 %reduce-scatter.11.cloned.1.call-done = f32[32,64]{1,0:T(8,128)} async-done(((f32[512,64]{1,0:T(8,128)}), f32[32,64]{1,0:T(8,128)}) %reduce-scatter.11.cloned.1.call-update) | async-done | bytes 8208 | tf_op jit(solution)/shard_map/reduce_scatter | solution.py:44
  668.8 19.8 %all_gather.15 = bf16[512,64]{1,0:T(8,128)(2,1)S(1)} all-gather(bf16[32,64]{1,0:T(8,128)(2,1)S(1)} %fusion.34), channel_id=1, replica_groups=mesh['prec'=16,'run'=2] {'prec'}, dimensions={0}, use_global_device_ids=true | all-gather | bytes 69632 | tf_op jit(solution)/shard_map/all_gather | solution.py:50
  693.5 8.3 %psum.94 = bf16[64,64]{0,1:T(8,128)(2,1)S(1)} all-reduce(bf16[64,64]{0,1:T(8,128)(2,1)S(1)} %convolution_convert_fusion.8), channel_id=1, replica_groups=mesh['prec'=16,'run'=2] {'run'}, use_global_device_ids=true, to_apply=%region_16.20 | all-reduce | flops 4096 | bytes 16384 | tf_op jit(solution)/shard_map/psum | solution.py:58
  701.9 5.8 cholesky.211
  713.9 19.1 %all-reduce.11.cloned.1.call-done = bf16[2048,64]{1,0:T(8,128)(2,1)} async-done(((bf16[2048,64]{1,0:T(8,128)(2,1)}), bf16[2048,64]{1,0:T(8,128)(2,1)}) %all-reduce.11.cloned.1.call-update) | async-done | bytes 262160 | tf_op jit(solution)/shard_map/psum | solution.py:57
  (122 shorter events, 92.3 us)
Async XLA Ops:
  6.5 9.4 %copy-start = (bf16[2048,64]{0,1:T(8,128)(2,1)S(1)}, bf16[2048,64]{0,1:T(8,128)(2,1)}, u32[]{:S(2)}) copy-start(bf16[2048,64]{0,1:T(8,128)(2,1)} %param.12) | copy-start | bytes 786436
  6.5 89.3 %reduce-scatter.5.cloned.1.call-start = ((), (), s32[]{:S(2)}) async-start(), calls=%async_computation.4 | async-start | bytes 278528 | tf_op jit(solution)/shard_map/reduce_scatter | solution.py:44
  10.3 5.7 copy-start.2
  10.3 5.7 copy-start.3
  20.4 134.4 %all-reduce.5.cloned.1.call-start = ((), (), s32[]{:S(2)}) async-start(), calls=%async_computation.5 | async-start | bytes 524288 | tf_op jit(solution)/shard_map/psum | solution.py:57
  133.5 148.0 %reduce-scatter.7.cloned.1.call-start = ((), (), s32[]{:S(2)}) async-start(), calls=%async_computation.6 | async-start | bytes 278528 | tf_op jit(solution)/shard_map/reduce_scatter | solution.py:44
  229.3 117.4 %all-reduce.7.cloned.1.call-start = ((), (), s32[]{:S(2)}) async-start(), calls=%async_computation.7 | async-start | bytes 1048576 | tf_op jit(solution)/shard_map/psum | solution.py:57
  321.6 152.8 %reduce-scatter.9.cloned.1.call-start = ((), (), s32[]{:S(2)}) async-start(), calls=%async_computation.8 | async-start | bytes 278528 | tf_op jit(solution)/shard_map/reduce_scatter | solution.py:44
  422.2 117.6 %all-reduce.9.cloned.1.call-start = ((), (), s32[]{:S(2)}) async-start(), calls=%async_computation.9 | async-start | bytes 1048576 | tf_op jit(solution)/shard_map/psum | solution.py:57
  514.7 152.8 %reduce-scatter.11.cloned.1.call-start = ((), (), s32[]{:S(2)}) async-start(), calls=%async_computation.10 | async-start | bytes 278528 | tf_op jit(solution)/shard_map/reduce_scatter | solution.py:44
  615.3 117.6 %all-reduce.11.cloned.1.call-start = ((), (), s32[]{:S(2)}) async-start(), calls=%async_computation.11 | async-start | bytes 1048576 | tf_op jit(solution)/shard_map/psum | solution.py:57
  733.0 3.4 copy-start.1
Sparse Core Ops, SparseCore 0:
  20.5 58.5 reduce-scatter.4
  133.6 21.0 all-reduce.4
  229.4 52.0 reduce-scatter.6
  321.7 24.9 all-reduce.6
  422.3 52.0 reduce-scatter.8
  514.8 24.9 all-reduce.8
  615.4 52.0 reduce-scatter.10
  708.0 24.9 all-reduce.10
where the time goes:
time: 755 us; the launch traced here: 746 us
  blocking collectives  356 us (47%)
  waiting for transfers between devices  212 us (28%)
  other arithmetic  96.2 us (13%)
  matrix products  57.4 us (8%)
  between operations  14.5 us (2%)
  local copies, waits for them, and re-layouts  10 us (1%)
    psum x4, blocking collectives, local(): gram_v = lax.psum(gram_part, 'prec')  246 us
    reduce_scatter x4, waiting for transfers between devices, local(): share = lax.psum_scatter(proj_part, 'prec', scatter_dimension=0, tiled=True)  140 us
    all_gather x4, blocking collectives, local(): u_now = lax.all_gather(fresh, 'prec', axis=0, tiled=True)  77 us
    psum x4, waiting for transfers between devices, local(): lax.psum(proj_part.astype(jnp.bfloat16), 'run').astype(jnp.float32)  72.2 us
    another operation x24, other arithmetic, ridge_solve(): jnp.linalg.cholesky(gram + ridge_value * jnp.eye(size, dtype=jnp.float32))  52.2 us
    another operation x16, other arithmetic, ridge_solve(): return jax.scipy.linalg.cho_solve((factor, True), matrix.T).T  43.9 us
    psum x4, blocking collectives, local(): lax.psum(gram_part.astype(jnp.bfloat16), 'run').astype(jnp.float32)  32.7 us
    dot_general x4, matrix products, local(): lax.dot_general(resid, u_now, (((0,), (0,)), ((), ())), preferred_element...  18.1 us
  transfers between devices with their start and end apart: 8, of which 7 were waited for; matrix products, arithmetic and copies ran while one was open for 7% of the time, Pallas kernels for 0%

commit v1 on v0

v1 whole, which is shorter than its diff:
```python
import functools

import jax
import jax.numpy as jnp
from jax import lax
from jax.experimental import pallas as pl
from jax.experimental.pallas import tpu as pltpu
from jax.sharding import PartitionSpec as P

ITERS = 4
ridge_value = 16.0
f32 = jnp.float32
bf16 = jnp.bfloat16
MESH = pl.DeviceIdType.MESH


def mm(a, b):
    return lax.dot_general(a, b, (((1,), (0,)), ((), ())), preferred_element_type=f32)


def mm_nt(a, b):
    return lax.dot_general(a, b, (((1,), (1,)), ((), ())), preferred_element_type=f32)


def spd_inverse(a):
    size = a.shape[0]
    wide = 2 * size
    rid = lax.broadcasted_iota(jnp.int32, (size, wide), 0)
    eye = (
        lax.broadcasted_iota(jnp.int32, (size, size), 0)
        == lax.broadcasted_iota(jnp.int32, (size, size), 1)
    ).astype(f32)
    m = jnp.concatenate([a + ridge_value * eye, eye], axis=1)
    group = 4
    for k0 in range(0, size, group):
        cols = [
            jnp.broadcast_to(m[:, k0 + j : k0 + j + 1], (size, wide)) for j in range(group)
        ]
        for j in range(group):
            k = k0 + j
            inv = 1.0 / cols[j][k : k + 1, :]
            prow = m[k : k + 1, :] * inv
            m = jnp.where(rid == k, prow, m - cols[j] * prow)
            for n in range(j + 1, group):
                f = cols[j][k0 + n : k0 + n + 1, :] * inv
                cols[n] = jnp.where(rid == k, f, cols[n] - cols[j] * f)
    return m[:, size:]


def split(x):
    hi = x.astype(bf16)
    return hi, (x - hi.astype(f32)).astype(bf16)


def pack_gram(g):
    h = g.shape[0] // 2
    return jnp.concatenate([g[:h], g[h:]], axis=1)


def unpack_gram(x):
    h = x.shape[1] // 2
    return jnp.concatenate([x[:, :h], x[:, h:]], axis=0)


def als_kernel(
    n, nr, fold, uchunks, vchunks,
    x_ref, w_ref, u0_ref, v0_ref, out_ref,
    mask, u, vt, gv, psend, precv, ub, gu, pv,
    gs, gr, ps, pr, us, ur, gus, gur, pvs, pvr,
):
    me = lax.axis_index("prec")
    my = lax.axis_index("run")
    rows, k = u0_ref.shape
    cols = x_ref.shape[1]
    sp = rows // n // fold
    rc = rows // uchunks
    cw = cols // vchunks
    per = n // uchunks
    others = [lax.rem(me + off, n) for off in range(1, n)]
    rothers = [lax.rem(my + off, nr) for off in range(1, nr)]

    barrier = pltpu.get_barrier_semaphore()
    for d in others:
        pl.semaphore_signal(barrier, inc=1, device_id={"prec": d}, device_id_type=MESH)
    for d in rothers:
        pl.semaphore_signal(barrier, inc=1, device_id={"run": d}, device_id_type=MESH)

    def rcopy(src, dst, ss, rs, axis, d):
        return pltpu.make_async_remote_copy(
            src_ref=src, dst_ref=dst, send_sem=ss, recv_sem=rs,
            device_id={axis: d}, device_id_type=MESH,
        )

    words = w_ref.shape[1]
    wb = min(128, words)
    spread = (
        lax.broadcasted_iota(jnp.int32, (wb, 8 * wb), 0)
        == lax.broadcasted_iota(jnp.int32, (wb, 8 * wb), 1) // 8
    ).astype(f32).astype(bf16)
    for c in range(words // wb):
        for r0 in range(0, rows, 128):
            part = w_ref[r0 : r0 + 128, c * wb : (c + 1) * wb].astype(f32).astype(bf16)
            wide = mm(part, spread).astype(jnp.int32)
            lane = lax.broadcasted_iota(jnp.int32, wide.shape, 1) & 7
            bit = lax.shift_right_logical(wide, lane) & 1
            mask[r0 : r0 + 128, c * 8 * wb : (c + 1) * 8 * wb] = bit.astype(f32).astype(bf16)

    u[...] = u0_ref[...]
    eye = (
        lax.broadcasted_iota(jnp.int32, (k, k), 0) == lax.broadcasted_iota(jnp.int32, (k, k), 1)
    ).astype(f32).astype(bf16)
    for c in range(vchunks):
        vt[:, c * cw : (c + 1) * cw] = mm_nt(eye, v0_ref[c * cw : (c + 1) * cw, :]).astype(bf16)

    def share_of(x, d):
        base = d * sp * fold
        parts = [x[base + f * sp : base + (f + 1) * sp, :] for f in range(fold)]
        return parts[0] if fold == 1 else jnp.concatenate(parts, axis=1)

    start = u0_ref[...].astype(f32)
    for d in range(n):
        ub[d] = share_of(start, d).astype(bf16)

    def resid(r0, r1, c0, c1, fit):
        m = mask[r0:r1, c0:c1].astype(f32)
        return (m * (x_ref[r0:r1, c0:c1].astype(f32) - fit)).astype(bf16)

    pl.semaphore_wait(barrier, n - 1 + nr - 1)

    def iteration(it, carry):
        par = lax.rem(it, 2)
        gv[me] = pack_gram(mm_nt(vt[...], vt[...]))
        for d in others:
            rcopy(gv.at[me], gv.at[me], gs.at[d], gr.at[me], "prec", d).start()
        for c in range(uchunks):
            r0, r1 = c * rc, (c + 1) * rc
            fit = mm(u[r0:r1, :], vt[...])
            proj = mm_nt(resid(r0, r1, 0, cols, fit), vt[...])
            for i in range(per):
                psend[c * per + i] = share_of(proj, i).astype(bf16)
            for i in range(per):
                d = c * per + i

                @pl.when(me != d)
                def _():
                    rcopy(psend.at[d], precv.at[me], ps.at[d], pr.at[me], "prec", d).start()

        for d in others:
            rcopy(gv.at[me], gv.at[d], gs.at[d], gr.at[d], "prec", d).wait_recv()
        total = gv[0]
        for d in range(1, n):
            total = total + gv[d]
        inv = spd_inverse(unpack_gram(total))
        for d in others:
            rcopy(psend.at[d], precv.at[d], ps.at[d], pr.at[d], "prec", d).wait_recv()
        share = psend[me].astype(f32)
        for d in others:
            share = share + precv[d].astype(f32)
        old = ub[me].astype(f32)
        dhi, dlo = split(share - ridge_value * old)
        ihi, ilo = split(inv)
        steps = []
        for f in range(fold):
            h, l = dhi[:, f * k : (f + 1) * k], dlo[:, f * k : (f + 1) * k]
            steps.append(mm(h, ihi) + mm(h, ilo) + mm(l, ihi))
        step = steps[0] if fold == 1 else jnp.concatenate(steps, axis=1)
        ub[me] = (old + step).astype(bf16)
        for d in others:
            rcopy(ub.at[me], ub.at[me], us.at[d], ur.at[me], "prec", d).start()
        for d in others:
            rcopy(gv.at[me], gv.at[d], gs.at[d], gr.at[d], "prec", d).wait_send()
            rcopy(psend.at[d], precv.at[d], ps.at[d], pr.at[d], "prec", d).wait_send()
        for d in others:
            rcopy(ub.at[me], ub.at[d], us.at[d], ur.at[d], "prec", d).wait()
        for d in range(n):
            base = d * sp * fold
            for f in range(fold):
                u[base + f * sp : base + (f + 1) * sp, :] = ub[d][:, f * k : (f + 1) * k]

        now = u[...]
        ut = mm_nt(eye, now).astype(bf16)
        gu[par, my] = pack_gram(mm_nt(ut, ut))
        for d in rothers:
            rcopy(gu.at[par, my], gu.at[par, my], gus.at[d], gur.at[par, my], "run", d).start()
        for c in range(vchunks):
            c0, c1 = c * cw, (c + 1) * cw
            fit = mm(now, vt[:, c0:c1])
            pv[par, my, c] = mm(ut, resid(0, rows, c0, c1, fit)).astype(bf16)
            for d in rothers:
                mine = pv.at[par, my, c]
                rcopy(mine, mine, pvs.at[d, c], pvr.at[par, my, c], "run", d).start()
        for d in rothers:
            rcopy(gu.at[par, my], gu.at[par, d], gus.at[d], gur.at[par, d], "run", d).wait()
        total = gu[par, 0]
        for d in range(1, nr):
            total = total + gu[par, d]
        ihi, ilo = split(spd_inverse(unpack_gram(total)))
        lhs = jnp.concatenate([ihi, ilo, ihi], axis=1)
        for c in range(vchunks):
            c0, c1 = c * cw, (c + 1) * cw
            for d in rothers:
                rcopy(
                    pv.at[par, my, c], pv.at[par, d, c], pvs.at[d, c], pvr.at[par, d, c], "run", d
                ).wait()
            share = pv[par, 0, c].astype(f32)
            for d in range(1, nr):
                share = share + pv[par, d, c].astype(f32)
            old = vt[:, c0:c1].astype(f32)
            dhi, dlo = split(share - ridge_value * old)
            step = mm(lhs, jnp.concatenate([dhi, dhi, dlo], axis=0))
            vt[:, c0:c1] = (old + step).astype(bf16)
        return carry

    lax.fori_loop(0, ITERS, iteration, 0)

    for c in range(vchunks):
        c0, c1 = c * cw, (c + 1) * cw
        fit = mm(u[...], vt[:, c0:c1])
        m = mask[:, c0:c1].astype(f32)
        out_ref[:, c0:c1] = (m * x_ref[:, c0:c1].astype(f32) + (1.0 - m) * fit).astype(bf16)


def local(n, nr, intensity, observed, run_factors, prec_factors):
    rows, cols = intensity.shape
    k = run_factors.shape[1]
    fold = 2 if rows // n % 32 == 0 else 1
    sp = rows // n // fold
    uchunks = 4
    vchunks = max(1, min(4, cols // 128))
    cw = cols // vchunks
    dma = pltpu.SemaphoreType.DMA
    vmem = pl.BlockSpec(memory_space=pltpu.VMEM)
    return pl.pallas_call(
        functools.partial(als_kernel, n, nr, fold, uchunks, vchunks),
        out_shape=jax.ShapeDtypeStruct((rows, cols), bf16),
        in_specs=[vmem] * 4,
        out_specs=vmem,
        scratch_shapes=[
            pltpu.VMEM((rows, cols), bf16),
            pltpu.VMEM((rows, k), bf16),
            pltpu.VMEM((k, cols), bf16),
            pltpu.VMEM((n, k // 2, 2 * k), f32),
            pltpu.VMEM((n, sp, k * fold), bf16),
            pltpu.VMEM((n, sp, k * fold), bf16),
            pltpu.VMEM((n, sp, k * fold), bf16),
            pltpu.VMEM((2, nr, k // 2, 2 * k), f32),
            pltpu.VMEM((2, nr, vchunks, k, cw), bf16),
            dma((n,)), dma((n,)), dma((n,)), dma((n,)), dma((n,)), dma((n,)),
            dma((nr,)), dma((2, nr)), dma((nr, vchunks)), dma((2, nr, vchunks)),
        ],
        compiler_params=pltpu.CompilerParams(
            collective_id=0, has_side_effects=True, vmem_limit_bytes=60 << 20
        ),
    )(intensity, observed, run_factors, prec_factors)


def solution(mesh):
    n, nr = mesh.shape["prec"], mesh.shape["run"]
    return jax.shard_map(
        functools.partial(local, n, nr),
        mesh=mesh,
        in_specs=(P("run", "prec"), P("run", "prec"), P("run", None), P("prec", None)),
        out_specs=P("run", "prec"),
        check_vma=False,
    )
```

time: 755 us -> 118 us (0.16); the launches traced: 746 us -> 118 us
  blocking collectives: 356 us -> 0 us
  waiting for transfers between devices: 212 us -> 0 us
  Pallas kernels: 0 us -> 111 us
  other arithmetic: 96.2 us -> 0 us
  matrix products: 57.4 us -> 0 us
  between operations: 14.5 us -> 0.01 us
    psum x8 -> x0, blocking collectives: 279 us -> none  [the longest x4 246 us: local(): gram_v = lax.psum(gram_part, 'prec')]
    reduce_scatter x4 -> x0, waiting for transfers between devices: 140 us -> none  [local(): share = lax.psum_scatter(proj_part, 'prec', scatter_dimension=0, tiled=True)]
    pallas_call x0 -> x1, Pallas kernels: none -> 111 us  [local(): pl.pallas_call(functools.partial(als_kernel, n, nr, fold, uchunks, vchunk...]
    another operation x40 -> x0, other arithmetic: 96 us -> none  [the longest x24 52.2 us: ridge_solve(): jnp.linalg.cholesky(gram + ridge_value * jnp.eye(size, dtype=jnp.float32))]
    all_gather x4 -> x0, blocking collectives: 77 us -> none  [local(): u_now = lax.all_gather(fresh, 'prec', axis=0, tiled=True)]
    psum x4 -> x0, waiting for transfers between devices: 72.2 us -> none  [local(): lax.psum(proj_part.astype(jnp.bfloat16), 'run').astype(jnp.float32)]
    dot_general x25 -> x0, matrix products: 48.7 us -> none  [the longest x4 18.1 us: local(): lax.dot_general(resid, u_now, (((0,), (0,)), ((), ())), preferred_element...]
    another operation x16 -> x0, matrix products: 8.67 us -> none  [ridge_solve(): return jax.scipy.linalg.cho_solve((factor, True), matrix.T).T]
  transfers between devices with their start and end apart: 8 -> 0, of which waited for: 7 -> 0; matrix products, arithmetic and copies ran while one was open for 7% -> 0% of each run, Pallas kernels for 0% -> 0%
where the time goes in v1:
time: 118 us
  Pallas kernels  111 us (94%)
  local copies, waits for them, and re-layouts  6.71 us (6%)
    pallas_call x1, Pallas kernels, local(): pl.pallas_call(functools.partial(als_kernel, n, nr, fold, uchunks, vchunk...  111 us
    unnamed x3, local copies, waits for them, and re-layouts  6.71 us

profile of v1, /device:TPU:0, one launch (start us, length us, event | category | flops | bytes accessed | tf_op | source)
XLA Modules:
  0.0 117.5 jit_solution(3054773955244000699)
XLA Ops:
  0.0 1.6 %copy.5.u0_ref = bf16[512,64]{1,0:T(8,128)(2,1)} copy(bf16[512,64]{0,1:T(8,128)(2,1)} %param.6) | data formatting | bytes 131072 | tf_op args[2]
  1.6 2.0 %copy.6.v0_ref = bf16[2048,64]{1,0:T(8,128)(2,1)} copy(bf16[2048,64]{0,1:T(8,128)(2,1)} %param.7) | data formatting | bytes 524288 | tf_op args[3]
  3.5 110.8 %shard_map.46 = bf16[512,2048]{1,0:T(8,128)(2,1)} custom-call(bf16[512,2048]{1,0:T(8,128)(2,1)} %x_ref.1, s32[512,256]{1,0:T(8,128)} %w_ref.1, bf16[512,64]{1,0:T(8,128)(2,1)} %copy.5.u0_ref, bf16[2048,64]{1,0:T(8,128)(2,1)} %copy.6.v0_ref), custom_call_target="tpu_custom_call" | custom-call | tf_op jit(solution)/shard_map/pallas_call | solution.py:233
  114.4 3.2 %copy.8 = bf16[512,2048]{1,0:T(8,128)(2,1)} copy(bf16[512,2048]{1,0:T(8,128)(2,1)} %shard_map.46) | data formatting | bytes 4194304

commit v2 on v1

--- a/solution.py
+++ b/solution.py
@@ -12,6 +12,7 @@
 f32 = jnp.float32
 bf16 = jnp.bfloat16
 MESH = pl.DeviceIdType.MESH
+VMEM_LIMIT = 32 << 20
 
 
 def mm(a, b):
@@ -63,22 +64,26 @@
 
 
 def als_kernel(
-    n, nr, fold, uchunks, vchunks,
-    x_ref, w_ref, u0_ref, v0_ref, out_ref,
-    mask, u, vt, gv, psend, precv, ub, gu, pv,
-    gs, gr, ps, pr, us, ur, gus, gur, pvs, pvr,
+    n, nr, group, fold, vchunks,
+    x_hbm, w_ref, ut0_ref, vt0_ref, out_ref,
+    x_ref, mask, u, vt, pacc, gv1, gv2, psend, precv, ub, gu, pv,
+    xs, g1s, g1r, g2s, g2r, ps, pr, us, ur, gus, gur, pvs, pvr,
 ):
     me = lax.axis_index("prec")
     my = lax.axis_index("run")
-    rows, k = u0_ref.shape
-    cols = x_ref.shape[1]
+    k, rows = ut0_ref.shape
+    cols = vt0_ref.shape[1]
     sp = rows // n // fold
-    rc = rows // uchunks
     cw = cols // vchunks
-    per = n // uchunks
+    planes = n // group
+    plane, seat = me // group, lax.rem(me, group)
     others = [lax.rem(me + off, n) for off in range(1, n)]
+    seats = [lax.rem(seat + off, group) for off in range(1, group)]
+    levels = [lax.rem(plane + off, planes) for off in range(1, planes)]
     rothers = [lax.rem(my + off, nr) for off in range(1, nr)]
 
+    load = pltpu.make_async_copy(x_hbm, x_ref, xs)
+    load.start()
     barrier = pltpu.get_barrier_semaphore()
     for d in others:
         pl.semaphore_signal(barrier, inc=1, device_id={"prec": d}, device_id_type=MESH)
@@ -105,60 +110,84 @@
             bit = lax.shift_right_logical(wide, lane) & 1
             mask[r0 : r0 + 128, c * 8 * wb : (c + 1) * 8 * wb] = bit.astype(f32).astype(bf16)
 
-    u[...] = u0_ref[...]
     eye = (
         lax.broadcasted_iota(jnp.int32, (k, k), 0) == lax.broadcasted_iota(jnp.int32, (k, k), 1)
     ).astype(f32).astype(bf16)
-    for c in range(vchunks):
-        vt[:, c * cw : (c + 1) * cw] = mm_nt(eye, v0_ref[c * cw : (c + 1) * cw, :]).astype(bf16)
 
     def share_of(x, d):
         base = d * sp * fold
         parts = [x[base + f * sp : base + (f + 1) * sp, :] for f in range(fold)]
         return parts[0] if fold == 1 else jnp.concatenate(parts, axis=1)
 
-    start = u0_ref[...].astype(f32)
+    start = jnp.transpose(ut0_ref[...].astype(f32))
+    u[...] = start.astype(bf16)
     for d in range(n):
         ub[d] = share_of(start, d).astype(bf16)
-
-    def resid(r0, r1, c0, c1, fit):
-        m = mask[r0:r1, c0:c1].astype(f32)
-        return (m * (x_ref[r0:r1, c0:c1].astype(f32) - fit)).astype(bf16)
-
-    pl.semaphore_wait(barrier, n - 1 + nr - 1)
-
-    def iteration(it, carry):
-        par = lax.rem(it, 2)
-        gv[me] = pack_gram(mm_nt(vt[...], vt[...]))
-        for d in others:
-            rcopy(gv.at[me], gv.at[me], gs.at[d], gr.at[me], "prec", d).start()
-        for c in range(uchunks):
-            r0, r1 = c * rc, (c + 1) * rc
-            fit = mm(u[r0:r1, :], vt[...])
-            proj = mm_nt(resid(r0, r1, 0, cols, fit), vt[...])
-            for i in range(per):
-                psend[c * per + i] = share_of(proj, i).astype(bf16)
-            for i in range(per):
-                d = c * per + i
-
-                @pl.when(me != d)
-                def _():
-                    rcopy(psend.at[d], precv.at[me], ps.at[d], pr.at[me], "prec", d).start()
-
-        for d in others:
-            rcopy(gv.at[me], gv.at[d], gs.at[d], gr.at[d], "prec", d).wait_recv()
-        total = gv[0]
-        for d in range(1, n):
-            total = total + gv[d]
-        inv = spd_inverse(unpack_gram(total))
-        for d in others:
-            rcopy(psend.at[d], precv.at[d], ps.at[d], pr.at[d], "prec", d).wait_recv()
+    vt[...] = vt0_ref[...]
+
+    def resid(c0, c1, fit):
+        m = mask[:, c0:c1].astype(f32)
+        return (m * (x_ref[:, c0:c1].astype(f32) - fit)).astype(bf16)
+
+    def g1(d):
+        return rcopy(gv1.at[seat], gv1.at[seat], g1s.at[d], g1r.at[seat], "prec", plane * group + d)
+
+    def g1_in(d):
+        return rcopy(gv1.at[seat], gv1.at[d], g1s.at[d], g1r.at[d], "prec", plane * group + d)
+
+    def g2(d):
+        return rcopy(gv2.at[plane], gv2.at[plane], g2s.at[d], g2r.at[plane], "prec", d * group + seat)
+
+    def g2_in(d):
+        return rcopy(gv2.at[plane], gv2.at[d], g2s.at[d], g2r.at[d], "prec", d * group + seat)
+
+    def p_out(d):
+        return rcopy(psend.at[d], precv.at[me], ps.at[d], pr.at[me], "prec", d)
+
+    def p_in(d):
+        return rcopy(psend.at[d], precv.at[d], ps.at[d], pr.at[d], "prec", d)
+
+    def launch_u(update):
+        gram = None
+        for c in range(vchunks):
+            c0, c1 = c * cw, (c + 1) * cw
+            if update is not None:
+                update(c)
+            v = vt[:, c0:c1]
+            gram = mm_nt(v, v) if gram is None else gram + mm_nt(v, v)
+            if c == vchunks - 1:
+                gv1[seat] = pack_gram(gram)
+                for d in seats:
+                    g1(d).start()
+            proj = mm_nt(resid(c0, c1, mm(u[...], v)), v)
+            pacc[...] = proj if c == 0 else pacc[...] + proj
+        for d in range(n):
+            psend[d] = share_of(pacc, d).astype(bf16)
+        for d in others:
+            p_out(d).start()
+
+    def finish_u():
+        for d in seats:
+            g1_in(d).wait_recv()
+        total = gv1[0]
+        for d in range(1, group):
+            total = total + gv1[d]
+        gv2[plane] = total
+        for d in levels:
+            g2(d).start()
+        for d in levels:
+            g2_in(d).wait_recv()
+        total = gv2[0]
+        for d in range(1, planes):
+            total = total + gv2[d]
+        ihi, ilo = split(spd_inverse(unpack_gram(total)))
+        for d in others:
+            p_in(d).wait_recv()
         share = psend[me].astype(f32)
         for d in others:
             share = share + precv[d].astype(f32)
         old = ub[me].astype(f32)
         dhi, dlo = split(share - ridge_value * old)
-        ihi, ilo = split(inv)
         steps = []
         for f in range(fold):
             h, l = dhi[:, f * k : (f + 1) * k], dlo[:, f * k : (f + 1) * k]
@@ -167,9 +196,12 @@
         ub[me] = (old + step).astype(bf16)
         for d in others:
             rcopy(ub.at[me], ub.at[me], us.at[d], ur.at[me], "prec", d).start()
-        for d in others:
-            rcopy(gv.at[me], gv.at[d], gs.at[d], gr.at[d], "prec", d).wait_send()
-            rcopy(psend.at[d], precv.at[d], ps.at[d], pr.at[d], "prec", d).wait_send()
+        for d in seats:
+            g1_in(d).wait_send()
+        for d in levels:
+            g2_in(d).wait_send()
+        for d in others:
+            p_in(d).wait_send()
         for d in others:
             rcopy(ub.at[me], ub.at[d], us.at[d], ur.at[d], "prec", d).wait()
         for d in range(n):
@@ -177,6 +209,7 @@
             for f in range(fold):
                 u[base + f * sp : base + (f + 1) * sp, :] = ub[d][:, f * k : (f + 1) * k]
 
+    def launch_v(par):
         now = u[...]
         ut = mm_nt(eye, now).astype(bf16)
         gu[par, my] = pack_gram(mm_nt(ut, ut))
@@ -185,7 +218,7 @@
         for c in range(vchunks):
             c0, c1 = c * cw, (c + 1) * cw
             fit = mm(now, vt[:, c0:c1])
-            pv[par, my, c] = mm(ut, resid(0, rows, c0, c1, fit)).astype(bf16)
+            pv[par, my, c] = mm(ut, resid(c0, c1, fit)).astype(bf16)
             for d in rothers:
                 mine = pv.at[par, my, c]
                 rcopy(mine, mine, pvs.at[d, c], pvr.at[par, my, c], "run", d).start()
@@ -196,7 +229,8 @@
             total = total + gu[par, d]
         ihi, ilo = split(spd_inverse(unpack_gram(total)))
         lhs = jnp.concatenate([ihi, ilo, ihi], axis=1)
-        for c in range(vchunks):
+
+        def update(c):
             c0, c1 = c * cw, (c + 1) * cw
             for d in rothers:
                 rcopy(
@@ -209,12 +243,24 @@
             dhi, dlo = split(share - ridge_value * old)
             step = mm(lhs, jnp.concatenate([dhi, dhi, dlo], axis=0))
             vt[:, c0:c1] = (old + step).astype(bf16)
+
+        return update
+
+    load.wait()
+    pl.semaphore_wait(barrier, n - 1 + nr - 1)
+    launch_u(None)
+
+    def iteration(it, carry):
+        finish_u()
+        launch_u(launch_v(lax.rem(it, 2)))
         return carry
 
-    lax.fori_loop(0, ITERS, iteration, 0)
-
+    lax.fori_loop(0, ITERS - 1, iteration, 0)
+    finish_u()
+    update = launch_v((ITERS - 1) % 2)
     for c in range(vchunks):
         c0, c1 = c * cw, (c + 1) * cw
+        update(c)
         fit = mm(u[...], vt[:, c0:c1])
         m = mask[:, c0:c1].astype(f32)
         out_ref[:, c0:c1] = (m * x_ref[:, c0:c1].astype(f32) + (1.0 - m) * fit).astype(bf16)
@@ -225,33 +271,40 @@
     k = run_factors.shape[1]
     fold = 2 if rows // n % 32 == 0 else 1
     sp = rows // n // fold
-    uchunks = 4
+    group = 1
+    while group * group * 4 <= n:
+        group *= 2
     vchunks = max(1, min(4, cols // 128))
     cw = cols // vchunks
     dma = pltpu.SemaphoreType.DMA
     vmem = pl.BlockSpec(memory_space=pltpu.VMEM)
     return pl.pallas_call(
-        functools.partial(als_kernel, n, nr, fold, uchunks, vchunks),
+        functools.partial(als_kernel, n, nr, group, fold, vchunks),
         out_shape=jax.ShapeDtypeStruct((rows, cols), bf16),
-        in_specs=[vmem] * 4,
+        in_specs=[pl.BlockSpec(memory_space=pl.ANY)] + [vmem] * 3,
         out_specs=vmem,
         scratch_shapes=[
             pltpu.VMEM((rows, cols), bf16),
+            pltpu.VMEM((rows, cols), bf16),
             pltpu.VMEM((rows, k), bf16),
             pltpu.VMEM((k, cols), bf16),
-            pltpu.VMEM((n, k // 2, 2 * k), f32),
+            pltpu.VMEM((rows, k), f32),
+            pltpu.VMEM((group, k // 2, 2 * k), f32),
+            pltpu.VMEM((n // group, k // 2, 2 * k), f32),
             pltpu.VMEM((n, sp, k * fold), bf16),
             pltpu.VMEM((n, sp, k * fold), bf16),
             pltpu.VMEM((n, sp, k * fold), bf16),
             pltpu.VMEM((2, nr, k // 2, 2 * k), f32),
             pltpu.VMEM((2, nr, vchunks, k, cw), bf16),
-            dma((n,)), dma((n,)), dma((n,)), dma((n,)), dma((n,)), dma((n,)),
+            dma(()),
+            dma((group,)), dma((group,)), dma((n // group,)), dma((n // group,)),
+            dma((n,)), dma((n,)), dma((n,)), dma((n,)),
             dma((nr,)), dma((2, nr)), dma((nr, vchunks)), dma((2, nr, vchunks)),
         ],
         compiler_params=pltpu.CompilerParams(
-            collective_id=0, has_side_effects=True, vmem_limit_bytes=60 << 20
+            collective_id=0, has_side_effects=True, vmem_limit_bytes=VMEM_LIMIT
         ),
-    )(intensity, observed, run_factors, prec_factors)
+    )(intensity, observed, run_factors.T, prec_factors.T)
 
 
 def solution(mesh):

time: 118 us -> 106 us (0.90)
  Pallas kernels: 111 us -> 100 us
    pallas_call x1, Pallas kernels: 111 us -> 100 us  [local(): pl.pallas_call(functools.partial(als_kernel, n, nr, group, fold, vchunks)...]
    unnamed x3 -> x9, local copies, waits for them, and re-layouts: 6.71 us -> 5.74 us
where the time goes in v2:
time: 106 us
  Pallas kernels  100 us (94%)
  local copies, waits for them, and re-layouts  5.74 us (5%)
    pallas_call x1, Pallas kernels, local(): pl.pallas_call(functools.partial(als_kernel, n, nr, group, fold, vchunks)...  100 us
    unnamed x9, local copies, waits for them, and re-layouts  5.74 us

profile of v2, /device:TPU:0, one launch (start us, length us, event | category | flops | bytes accessed | tf_op | source)
XLA Modules:
  0.0 106.1 jit_solution(9757859891654119306)
XLA Ops:
  0.0 0.0 copy-start
  0.0 1.6 %copy-done = bf16[512,2048]{1,0:T(8,128)(2,1)S(1)} copy-done((bf16[512,2048]{1,0:T(8,128)(2,1)S(1)}, bf16[512,2048]{1,0:T(8,128)(2,1)}, u32[]{:S(2)}) %copy-start) | copy-done | bytes 2097176
  1.6 0.0 copy-start.1
  1.6 1.0 copy-done.1
  2.6 0.0 copy-start.2
  2.6 0.9 copy-done.2
  3.6 0.0 copy-start.3
  3.6 0.8 copy-done.3
  4.4 100.3 %shard_map.46 = bf16[512,2048]{1,0:T(8,128)(2,1)S(1)} custom-call(bf16[512,2048]{1,0:T(8,128)(2,1)S(1)} %copy-done, s32[512,256]{1,0:T(8,128)S(1)} %copy-done.1, bf16[64,512]{1,0:T(8,128)(2,1)S(1)} %bitcast.3, bf16[64,2048]{1,0:T(8,128)(2,1)S(1)} %bitcast.2), custom_call_target="tpu_custom_call" | custom-call | tf_op jit(solution)/shard_map/pallas_call | solution.py:281
  104.8 1.3 %copy.6 = bf16[512,2048]{1,0:T(8,128)(2,1)} copy(bf16[512,2048]{1,0:T(8,128)(2,1)S(1)} %shard_map.46) | data formatting | bytes 4194304
Async XLA Ops:
  0.0 1.6 %copy-start = (bf16[512,2048]{1,0:T(8,128)(2,1)S(1)}, bf16[512,2048]{1,0:T(8,128)(2,1)}, u32[]{:S(2)}) copy-start(bf16[512,2048]{1,0:T(8,128)(2,1)} %x_hbm.1) | copy-start | bytes 6291460
  1.6 1.0 copy-start.1
  2.6 0.9 copy-start.2
  3.6 0.8 copy-start.3
